TPU v7x, 32 devices: a whole 2x2x4 slice. The times are simulated.
32 devices in a mesh: row: 4 (over y, x), orb: 8 (over z, core).
Axes of the slice: x: 2, y: 2, z: 4, core: 2. Of those that a mesh axis runs over, the one named last changes fastest.
Arguments:
- integrals: bfloat16 [24, 1024, 5120], P('orb', 'row'), may hold values from -6 to 6
- tile_ids: int32 [8, 40], P('row'), may hold values from 0 to 127, as said below
- coefficients: bfloat16 [1024, 16384], P('orb'), may hold values from -0.078125 to 0.078125
- metric: float32 [24, 24], replicated, may hold values from -0.0078125 to 0.0078125
Outputs:
- exchange_columns: float32 [1024, 1024], P('orb', 'row')
Inputs may be any that keep to these rules, and one draw needn't show every extreme that they name: `tile_ids`: row block b covers basis functions b * 128 to b * 128 + 127. Each row lists 40 different column tiles (tile t covers basis functions t * 128 to t * 128 + 127); the first is the block's own tile b.
All inputs are finite; a program needn't handle non-finite values.
Results may differ from a plain program's by a relative error of at most 0.022.
Values may be sent and summed in bfloat16 or wider, within the bound.
A program may use at most 128 MiB of HBM per device.

v0:
```python
import jax
import jax.numpy as jnp
from jax import lax
from jax.sharding import PartitionSpec as P


def per_device(integrals, tile_ids, coefficients, metric):
    aux_local, local_rows, kept_width = integrals.shape
    orb_local, basis_width = coefficients.shape
    block_count, kept_count = tile_ids.shape
    tile_rows = local_rows // block_count
    blocked = coefficients.reshape(orb_local, basis_width // tile_rows, tile_rows)
    picked = jnp.take(blocked, tile_ids.reshape(block_count * kept_count), axis=1)
    picked = picked.reshape(orb_local, block_count, kept_count * tile_rows)
    slabs = integrals.reshape(aux_local, block_count, tile_rows, kept_width)
    col_piece = lax.all_gather(picked, "orb", axis=0, tiled=True)
    halves = jnp.einsum("pbmk,jbk->pjbm", slabs, col_piece, preferred_element_type=jnp.float32)
    halves = halves.reshape(aux_local, col_piece.shape[0], local_rows).astype(jnp.bfloat16)
    own_piece = col_piece[:, :, :tile_rows].reshape(col_piece.shape[0], local_rows)
    stacked = jnp.concatenate([halves, own_piece[None]], axis=0)
    halves = stacked[:aux_local]
    own_rows = stacked[aux_local]
    by_orbital = lax.all_to_all(halves, "orb", split_axis=1, concat_axis=0, tiled=True)
    partial_sum = jnp.einsum(
        "qjm,im->qji", by_orbital, own_rows, preferred_element_type=jnp.float32
    )
    occupied_share = lax.psum_scatter(
        partial_sum.astype(jnp.bfloat16), "row", scatter_dimension=2, tiled=True
    ).astype(jnp.float32)
    fitted_share = jnp.einsum(
        "pq,qji->pji", metric, occupied_share, precision=lax.Precision.HIGHEST
    ).astype(jnp.bfloat16)
    fitted = lax.all_gather(fitted_share, "row", axis=2, tiled=True)
    return lax.psum_scatter(
        jnp.einsum("pjm,pji->im", by_orbital, fitted, preferred_element_type=jnp.float32).astype(
            jnp.bfloat16
        ),
        "orb",
        scatter_dimension=0,
        tiled=True,
    ).astype(jnp.float32)


def solution(mesh):
    return jax.shard_map(
        per_device,
        mesh=mesh,
        in_specs=(P("orb", "row", None), P("row", None), P("orb", None), P()),
        out_specs=P("orb", "row"),
        check_vma=False,
    )
```

profile of v0, /device:TPU:0, one launch (start us, length us, event | category | flops | bytes accessed | tf_op | source)
XLA Modules:
  0.0 483.4 jit_solution(17122439805342675751)
XLA Ops:
  6.5 0.0 copy-start
  6.5 0.0 all-gather.3.cloned.1.call-start
  6.5 0.8 reshape.51
  7.3 0.7 compare_and_fusion
  8.0 0.1 broadcast_bitcast_fusion
  8.1 6.4 %copy.25 = bf16[128,16384]{0,1:T(8,128)(2,1)} copy(bf16[128,16384]{1,0:T(8,128)(2,1)} %param.6) | data formatting | bytes 8388608 | tf_op args[2]
  14.5 6.4 %copy.26 = bf16[128,128,128]{2,0,1:T(8,128)(2,1)} copy(bf16[128,128,128]{0,2,1:T(8,128)(2,1)} %bitcast.42) | data formatting | bytes 8388608 | tf_op jit(solution)/shard_map/reshape | solution.py:12
  20.9 3.2 gather_fusion
  24.2 2.6 copy.27
  26.7 3.0 copy.28
  29.7 1.8 broadcast_select_fusion
  31.5 0.0 all-gather.3.cloned.1.call-update
  31.6 188.3 %all-gather.3.cloned.1.call-done = bf16[1024,2,5120]{2,0,1:T(8,128)(2,1)} async-done(((bf16[128,2,5120]{2,0,1:T(8,128)(2,1)}), bf16[1024,2,5120]{2,0,1:T(8,128)(2,1)}) %all-gather.3.cloned.1.call-update) | async-done | bytes 20971536 | tf_op jit(solution)/shard_map/all_gather | solution.py:16
  219.9 14.0 %fusion.11 = bf16[3,1024,2,128]{1,3,0,2:T(8,128)(2,1)S(1)} fusion(bf16[3,2,128,5120]{3,2,1,0:T(8,128)(2,1)} %bitcast.51, bf16[1024,2,5120]{2,0,1:T(8,128)(2,1)} %all-gather.3.cloned.1.call-done), kind=kOutput, calls=%fused_computation.11 | convolution fusion | flops 8053850112 | bytes 30408704 | tf_op jit(solution)/shard_map/pbmk,jbk->pjbm/dot_general | solution.py:17
  233.9 0.2 copy.30
  234.1 2.6 copy.31
  236.6 0.0 slice-start
  236.6 3.7 all-to-all-start
  240.4 0.0 reduce-scatter.3.cloned.1.call-start
  240.4 0.0 slice-done
  240.4 0.2 copy.34
  240.7 48.7 %all-to-all-done = bf16[3,1024,256]{2,0,1:T(4,128)(2,1)S(1)} async-done(((bf16[3,1024,256]{2,0,1:T(4,128)(2,1)}), bf16[3,1024,256]{2,0,1:T(4,128)(2,1)S(1)}, u32[]{:S(2)}, u32[]{:S(2)}) %all-to-all-start) | async-done | bytes 1572896 | tf_op jit(solution)/shard_map/all_to_all | solution.py:23
  289.3 0.2 copy.32
  289.6 0.1 copy.33
  289.7 4.5 convolution_convert_fusion
  294.1 0.0 reduce-scatter.3.cloned.1.call-update
  294.2 0.0 all-gather.5.cloned.1.call-start
  294.2 69.0 %reduce-scatter.3.cloned.1.call-done = bf16[24,128,256]{2,1,0:T(8,128)(2,1)} async-done(((bf16[24,128,1024]{2,1,0:T(8,128)(2,1)}), bf16[24,128,256]{2,1,0:T(8,128)(2,1)}) %reduce-scatter.3.cloned.1.call-update) | async-done | bytes 1572880 | tf_op jit(solution)/shard_map/reduce_scatter | solution.py:27
  363.2 0.0 copy-done
  363.2 4.5 fusion.16
  367.7 0.0 all-gather.5.cloned.1.call-update
  367.7 0.0 reduce-scatter.5.cloned.1.call-start
  367.8 70.0 %all-gather.5.cloned.1.call-done = bf16[24,128,1024]{2,0,1:T(8,128)(2,1)} async-done(((bf16[24,128,256]{2,0,1:T(8,128)(2,1)}), bf16[24,128,1024]{2,0,1:T(8,128)(2,1)}) %all-gather.5.cloned.1.call-update) | async-done | bytes 6291472 | tf_op jit(solution)/shard_map/all_gather | solution.py:33
  437.8 6.0 %fusion.22 = bf16[1024,256]{1,0:T(8,128)(2,1)} fusion(bf16[24,128,1024]{2,0,1:T(8,128)(2,1)} %all-gather.5.cloned.1.call-done, bf16[24,128,256]{2,1,0:T(8,128)(2,1)S(1)} %bitcast.46), kind=kOutput, calls=%fused_computation.14 | convolution fusion | flops 1610874880 | bytes 8388608 | tf_op jit(solution)/shard_map/pjm,pji->im/dot_general | solution.py:35
  443.8 0.0 reduce-scatter.5.cloned.1.call-update
  443.8 31.6 %reduce-scatter.5.cloned.1.call-done = bf16[128,256]{1,0:T(8,128)(2,1)} async-done(((bf16[1024,256]{1,0:T(8,128)(2,1)}), bf16[128,256]{1,0:T(8,128)(2,1)}) %reduce-scatter.5.cloned.1.call-update) | async-done | bytes 65552 | tf_op jit(solution)/shard_map/reduce_scatter | solution.py:34
  475.4 1.5 convert_element_type.32
  (3 shorter events, 0.0 us)
Async XLA Ops:
  6.5 356.6 %copy-start = (f32[24,24]{1,0:T(8,128)S(1)}, f32[24,24]{1,0:T(8,128)}, u32[]{:S(2)}) copy-start(f32[24,24]{1,0:T(8,128)} %param.7) | copy-start | bytes 6916
  6.5 213.4 %all-gather.3.cloned.1.call-start = ((), (), s32[]{:S(2)}) async-start(), calls=%async_computation.3 | async-start | bytes 23592960 | tf_op jit(solution)/shard_map/all_gather | solution.py:16
  236.6 3.8 slice-start
  236.6 52.7 %all-to-all-start = ((bf16[3,1024,256]{2,0,1:T(4,128)(2,1)}), bf16[3,1024,256]{2,0,1:T(4,128)(2,1)S(1)}, u32[]{:S(2)}, u32[]{:S(2)}) async-start(bf16[3,1024,256]{2,0,1:T(4,128)(2,1)} %copy.31), calls=%async_computation | async-start | bytes 4194304 | tf_op jit(solution)/shard_map/all_to_all | solution.py:23
  240.4 122.8 %reduce-scatter.3.cloned.1.call-start = ((), (), s32[]{:S(2)}) async-start(), calls=%async_computation.4 | async-start | bytes 7864320 | tf_op jit(solution)/shard_map/reduce_scatter | solution.py:27
  294.2 143.6 %all-gather.5.cloned.1.call-start = ((), (), s32[]{:S(2)}) async-start(), calls=%async_computation.5 | async-start | bytes 7864320 | tf_op jit(solution)/shard_map/all_gather | solution.py:33
  367.7 107.6 %reduce-scatter.5.cloned.1.call-start = ((), (), s32[]{:S(2)}) async-start(), calls=%async_computation.6 | async-start | bytes 589824 | tf_op jit(solution)/shard_map/reduce_scatter | solution.py:34
Sparse Core Ops, SparseCore 0:
  31.7 188.1 all-gather.2
  294.3 68.8 reduce-scatter.2
  367.8 69.8 all-gather.4
  443.9 31.4 reduce-scatter.4
where the time goes:
time: 484 us; the launch traced here: 483 us
  waiting for transfers between devices  408 us (84%)
  matrix products  28.9 us (6%)
  local copies, waits for them, and re-layouts  25.8 us (5%)
  between operations  13.2 us (3%)
    all_gather x1, waiting for transfers between devices, per_device(): col_piece = lax.all_gather(picked, 'orb', axis=0, tiled=True)  188 us
    all_gather x1, waiting for transfers between devices, per_device(): fitted = lax.all_gather(fitted_share, 'row', axis=2, tiled=True)  70 us
    reduce_scatter x1, waiting for transfers between devices, per_device(): lax.psum_scatter(partial_sum.astype(jnp.bfloat16), 'row', scatter_dimensi...  69 us
    all_to_all x1, waiting for transfers between devices, per_device(): lax.all_to_all(halves, 'orb', split_axis=1, concat_axis=0, tiled=True)  48.7 us
    reduce_scatter x1, waiting for transfers between devices, per_device(): lax.psum_scatter(jnp.einsum('pjm,pji->im', by_orbital, fitted, preferred_...  31.6 us
    dot_general x1, matrix products, per_device(): jnp.einsum('pbmk,jbk->pjbm', slabs, col_piece, preferred_element_type=jnp...  14 us
  transfers between devices with their start and end apart: 5, of which 5 were waited for; matrix products, arithmetic and copies ran while one was open for 0% of the time, Pallas kernels for 0%

commit v1 on v0

--- a/solution.py
+++ b/solution.py
@@ -20,7 +20,10 @@
     stacked = jnp.concatenate([halves, own_piece[None]], axis=0)
     halves = stacked[:aux_local]
     own_rows = stacked[aux_local]
-    by_orbital = lax.all_to_all(halves, "orb", split_axis=1, concat_axis=0, tiled=True)
+    by_orbital = jnp.concatenate(
+        lax.all_to_all(jnp.stack(jnp.split(halves, lax.axis_size("orb"), axis=1)), "orb", 0, 0),
+        axis=0,
+    )
     partial_sum = jnp.einsum(
         "qjm,im->qji", by_orbital, own_rows, preferred_element_type=jnp.float32
     )

time: 484 us -> 475 us (0.981)
  waiting for transfers between devices: 408 us -> 395 us
    all_to_all x1, waiting for transfers between devices: 48.7 us -> 37.4 us  [per_device(): lax.all_to_all(jnp.stack(jnp.split(halves, lax.axis_size('orb'), axis=1))...]
    unnamed x5 -> x12, local copies, waits for them, and re-layouts: 6.48 us -> 11.6 us
where the time goes in v1:
time: 475 us
  waiting for transfers between devices  395 us (83%)
  local copies, waits for them, and re-layouts  29.8 us (6%)
  matrix products  28.4 us (6%)
  between operations  13.2 us (3%)
    all_gather x1, waiting for transfers between devices, per_device(): col_piece = lax.all_gather(picked, 'orb', axis=0, tiled=True)  188 us
    reduce_scatter x1, waiting for transfers between devices, per_device(): lax.psum_scatter(partial_sum.astype(jnp.bfloat16), 'row', scatter_dimensi...  69 us
    all_gather x1, waiting for transfers between devices, per_device(): fitted = lax.all_gather(fitted_share, 'row', axis=2, tiled=True)  68.7 us
    all_to_all x1, waiting for transfers between devices, per_device(): lax.all_to_all(jnp.stack(jnp.split(halves, lax.axis_size('orb'), axis=1))...  37.4 us
    reduce_scatter x1, waiting for transfers between devices, per_device(): lax.psum_scatter(jnp.einsum('pjm,pji->im', by_orbital, fitted, preferred_...  31.6 us
    dot_general x1, matrix products, per_device(): jnp.einsum('pbmk,jbk->pjbm', slabs, col_piece, preferred_element_type=jnp...  14 us
    unnamed x12, local copies, waits for them, and re-layouts  11.6 us
  transfers between devices with their start and end apart: 5, of which 5 were waited for; matrix products, arithmetic and copies ran while one was open for 0% of the time, Pallas kernels for 0%

profile of v1, /device:TPU:0, one launch (start us, length us, event | category | flops | bytes accessed | tf_op | source)
XLA Modules:
  0.0 474.5 jit_solution(1691613782057357635)
XLA Ops:
  6.5 0.0 copy-start
  6.5 0.0 all-gather.3.cloned.1.call-start
  6.5 0.8 reshape.54
  7.3 0.7 compare_and_fusion
  8.0 0.1 broadcast_bitcast_fusion
  8.1 6.4 %copy.12 = bf16[128,16384]{0,1:T(8,128)(2,1)} copy(bf16[128,16384]{1,0:T(8,128)(2,1)} %param.6) | data formatting | bytes 8388608 | tf_op args[2]
  14.5 6.4 %copy.13 = bf16[128,128,128]{2,0,1:T(8,128)(2,1)} copy(bf16[128,128,128]{0,2,1:T(8,128)(2,1)} %bitcast.74) | data formatting | bytes 8388608 | tf_op jit(solution)/shard_map/reshape | solution.py:12
  20.9 3.2 gather_fusion
  24.2 2.6 copy.14
  26.7 3.0 copy.15
  29.7 1.8 broadcast_select_fusion
  31.5 0.0 all-gather.3.cloned.1.call-update
  31.6 188.3 %all-gather.3.cloned.1.call-done = bf16[1024,2,5120]{2,0,1:T(8,128)(2,1)} async-done(((bf16[128,2,5120]{2,0,1:T(8,128)(2,1)}), bf16[1024,2,5120]{2,0,1:T(8,128)(2,1)}) %all-gather.3.cloned.1.call-update) | async-done | bytes 20971536 | tf_op jit(solution)/shard_map/all_gather | solution.py:16
  219.9 14.0 %fusion.9 = bf16[3,1024,2,128]{1,3,0,2:T(8,128)(2,1)S(1)} fusion(bf16[3,2,128,5120]{3,2,1,0:T(8,128)(2,1)} %bitcast.89, bf16[1024,2,5120]{2,0,1:T(8,128)(2,1)} %all-gather.3.cloned.1.call-done), kind=kOutput, calls=%fused_computation.9 | convolution fusion | flops 8053850112 | bytes 30408704 | tf_op jit(solution)/shard_map/pbmk,jbk->pjbm/dot_general | solution.py:17
  233.9 0.1 copy.17
  234.0 0.7 fusion.25
  234.7 0.7 fusion.24
  235.5 0.7 fusion.23
  236.2 0.7 fusion.22
  236.9 0.7 fusion.21
  237.6 0.7 fusion.20
  238.4 0.7 fusion.19
  239.1 0.7 fusion.18
  239.8 0.0 slice-start
  239.8 3.7 all-to-all-start
  243.6 0.0 reduce-scatter.3.cloned.1.call-start
  243.6 0.0 slice-done
  243.6 0.2 copy.19
  243.9 37.4 %all-to-all-done = bf16[8,3,128,256]{2,3,1,0:T(8,128)(2,1)S(1)} async-done(((bf16[8,3,128,256]{2,3,1,0:T(8,128)(2,1)}), bf16[8,3,128,256]{2,3,1,0:T(8,128)(2,1)S(1)}, u32[]{:S(2)}, u32[]{:S(2)}) %all-to-all-start) | async-done | bytes 1572896 | tf_op jit(solution)/shard_map/all_to_all | solution.py:24
  281.3 4.5 convolution_convert_fusion
  285.8 0.0 reduce-scatter.3.cloned.1.call-update
  285.8 0.0 all-gather.5.cloned.1.call-start
  285.9 69.0 %reduce-scatter.3.cloned.1.call-done = bf16[24,128,256]{2,1,0:T(8,128)(2,1)} async-done(((bf16[24,128,1024]{2,1,0:T(8,128)(2,1)}), bf16[24,128,256]{2,1,0:T(8,128)(2,1)}) %reduce-scatter.3.cloned.1.call-update) | async-done | bytes 1572880 | tf_op jit(solution)/shard_map/reduce_scatter | solution.py:30
  354.8 0.0 copy-done
  354.8 4.5 fusion.14
  359.3 0.0 all-gather.5.cloned.1.call-update
  359.4 0.2 reduce-scatter.5.cloned.1.call-start
  359.6 1.1 copy.26
  360.7 68.7 %all-gather.5.cloned.1.call-done = bf16[24,128,1024]{2,0,1:T(8,128)(2,1)} async-done(((bf16[24,128,256]{2,0,1:T(8,128)(2,1)}), bf16[24,128,1024]{2,0,1:T(8,128)(2,1)}) %all-gather.5.cloned.1.call-update) | async-done | bytes 6291472 | tf_op jit(solution)/shard_map/all_gather | solution.py:36
  429.4 5.5 %fusion.17 = bf16[1024,256]{1,0:T(8,128)(2,1)} fusion(bf16[24,128,1024]{2,0,1:T(8,128)(2,1)} %all-gather.5.cloned.1.call-done, bf16[24,128,256]{2,0,1:T(8,128)(2,1)S(1)} %copy.26), kind=kOutput, calls=%fused_computation.12 | convolution fusion | flops 1610874880 | bytes 8388608 | tf_op jit(solution)/shard_map/pjm,pji->im/dot_general | solution.py:38
  434.9 0.0 reduce-scatter.5.cloned.1.call-update
  434.9 31.6 %reduce-scatter.5.cloned.1.call-done = bf16[128,256]{1,0:T(8,128)(2,1)} async-done(((bf16[1024,256]{1,0:T(8,128)(2,1)}), bf16[128,256]{1,0:T(8,128)(2,1)}) %reduce-scatter.5.cloned.1.call-update) | async-done | bytes 65552 | tf_op jit(solution)/shard_map/reduce_scatter | solution.py:37
  466.5 1.5 convert_element_type.32
  (3 shorter events, 0.0 us)
Async XLA Ops:
  6.5 348.3 %copy-start = (f32[24,24]{1,0:T(8,128)S(1)}, f32[24,24]{1,0:T(8,128)}, u32[]{:S(2)}) copy-start(f32[24,24]{1,0:T(8,128)} %param.7) | copy-start | bytes 6916
  6.5 213.4 %all-gather.3.cloned.1.call-start = ((), (), s32[]{:S(2)}) async-start(), calls=%async_computation.3 | async-start | bytes 23592960 | tf_op jit(solution)/shard_map/all_gather | solution.py:16
  239.8 3.8 slice-start
  239.8 41.4 %all-to-all-start = ((bf16[8,3,128,256]{2,3,1,0:T(8,128)(2,1)}), bf16[8,3,128,256]{2,3,1,0:T(8,128)(2,1)S(1)}, u32[]{:S(2)}, u32[]{:S(2)}) async-start(bf16[8,3,128,256]{2,3,1,0:T(8,128)(2,1)} %fusion.18), calls=%async_computation | async-start | bytes 3145728 | tf_op jit(solution)/shard_map/all_to_all | solution.py:24
  243.6 111.3 %reduce-scatter.3.cloned.1.call-start = ((), (), s32[]{:S(2)}) async-start(), calls=%async_computation.4 | async-start | bytes 7864320 | tf_op jit(solution)/shard_map/reduce_scatter | solution.py:30
  285.8 143.6 %all-gather.5.cloned.1.call-start = ((), (), s32[]{:S(2)}) async-start(), calls=%async_computation.5 | async-start | bytes 7864320 | tf_op jit(solution)/shard_map/all_gather | solution.py:36
  359.4 107.1 %reduce-scatter.5.cloned.1.call-start = ((), (), s32[]{:S(2)}) async-start(), calls=%async_computation.6 | async-start | bytes 589824 | tf_op jit(solution)/shard_map/reduce_scatter | solution.py:37
Sparse Core Ops, SparseCore 0:
  31.7 188.1 all-gather.2
  285.9 68.8 reduce-scatter.2
  359.5 69.8 all-gather.4
  435.0 31.3 reduce-scatter.4
